TPU v7x, 32 devices: a whole 2x2x4 slice. The times are simulated.
32 devices in a mesh: seq: 4 (over y, x), fsdp: 8 (over z, core).
Axes of the slice: x: 2, y: 2, z: 4, core: 2. Of those that a mesh axis runs over, the one named last changes fastest.
Arguments:
- hidden_in: bfloat16 [8, 1024, 1024], P('fsdp', 'seq'), may hold values from -10 to 10
- segment_ids: int32 [8, 1024], P('fsdp'), may hold values from 0 to 2, never falling along the last dimension, each value on 1 to 768 neighbouring positions
- valid_tokens: int32 [8, 1024], P('fsdp'), may hold values from 0 to 1
- w_qkv: bfloat16 [1024, 3072], P('fsdp'), may hold values from -0.1875 to 0.1875
- w_attn_out: bfloat16 [1024, 1024], P('fsdp'), may hold values from -2 to 2
- w_in_proj: bfloat16 [1024, 5248], P('fsdp'), may hold values from -0.1875 to 0.1875
- w_out_proj: bfloat16 [2624, 1024], P('fsdp'), may hold values from -0.125 to 0.125
- attn_gain: bfloat16 [1024], P('fsdp'), may hold values from 0.25 to 1.75
- mlp_gain: bfloat16 [1024], P('fsdp'), may hold values from 0.25 to 1.75
- cotangent: bfloat16 [8, 1024, 1024], P('fsdp', 'seq'), may hold values from -6 to 6
Outputs:
- hidden_out: bfloat16 [8, 1024, 1024], P('fsdp', 'seq')
- grad_in: float32 [8, 1024, 1024], P('fsdp', 'seq')
- grad_qkv: float32 [1024, 3072], P('fsdp')
- grad_attn_out: float32 [1024, 1024], P('fsdp')
- grad_in_proj: float32 [1024, 5248], P('fsdp')
- grad_out_proj: float32 [2624, 1024], P('fsdp')
- grad_attn_gain: float32 [1024], P('fsdp')
- grad_mlp_gain: float32 [1024], P('fsdp')
- rms_values: float32 [3], replicated
All inputs are finite; a program needn't handle non-finite values.
Results may differ from a plain program's by a relative error of at most 0.014.
The roundings to bfloat16 on the way count: a program that leaves them out, or rounds other values in their place, can miss the bound.
Values may be sent and summed in bfloat16 or wider, within the bound.
No kernel may reach another device: no remote copies, remote signals or barrier semaphores. Data moves between devices by JAX's collectives and lax.ppermute only.
A program may use at most 192 MiB of HBM per device.

v0:
```python
import jax
import jax.numpy as jnp
from jax import lax
from jax.sharding import PartitionSpec as P

D = 1024
HEADS = 16
HD = 64
FF = 2624
ROPE_BASE = 160000.0
NORM_EPS = 1e-05


def norm_rows(values, gain_row):
    average = jnp.mean(values, axis=-1, keepdims=True)
    centered = values - average
    variance = jnp.mean(centered * centered, axis=-1, keepdims=True)
    return centered * lax.rsqrt(variance + NORM_EPS) * gain_row


def rotate(head_values, positions):
    half_width = head_values.shape[-1] // 2
    frequency = ROPE_BASE ** (
        -2.0 * jnp.arange(half_width, dtype=jnp.float32) / head_values.shape[-1]
    )
    angles = positions.astype(jnp.float32)[:, None] * frequency[None, :]
    cosine = jnp.cos(angles)[:, None, :]
    sine_part = jnp.sin(angles)[:, None, :]
    first_half = head_values[..., :half_width]
    second = head_values[..., half_width:]
    return jnp.concatenate(
        [first_half * cosine - second * sine_part, second * cosine + first_half * sine_part],
        axis=-1,
    )


def gelu_gate(inputs, gates):
    return 0.5 * inputs * (1.0 + jax.scipy.special.erf(inputs * 0.7071067811865476)) * gates


def allowed_mask(seg_block, row_ids, seg_all, valid_all):
    col_ids = jnp.arange(seg_all.shape[0], dtype=jnp.int32)
    return (seg_block[:, None] == seg_all[None, :]) & (
        (valid_all[None, :] > 0) | (row_ids[:, None] == col_ids[None, :])
    )


def attend_forward(queries, key_heads, value_heads, seg_all, valid_all):
    length, head_local, head_width = queries.shape
    block_rows = min(512, length)
    block_count = length // block_rows
    score_scale = float(head_width) ** (-0.5)
    row_ids = jnp.arange(length, dtype=jnp.int32).reshape(block_count, block_rows)

    def one_block(block_items):
        query_block, seg_block, row_block = block_items
        scores = (
            jnp.einsum("qhd,khd->hqk", query_block, key_heads, preferred_element_type=jnp.float32)
            * score_scale
        )
        allowed = allowed_mask(seg_block, row_block, seg_all, valid_all)[None]
        scores = jnp.where(allowed, scores, -1e30)
        row_max = jnp.max(scores, axis=-1, keepdims=True)
        exponent = jnp.exp(scores - row_max)
        denominator = jnp.sum(exponent, axis=-1, keepdims=True)
        weights = (exponent / denominator).astype(jnp.bfloat16)
        output = jnp.einsum(
            "hqk,khd->qhd", weights, value_heads, preferred_element_type=jnp.float32
        )
        return (output, (row_max + jnp.log(denominator))[..., 0])

    outputs, log_sums = lax.map(
        one_block,
        (
            queries.reshape(block_count, block_rows, head_local, head_width),
            seg_all.reshape(block_count, block_rows),
            row_ids,
        ),
    )
    return (outputs.reshape(length, head_local, head_width), log_sums)


def attend_backward(queries, key_heads, value_heads, grad_out, log_sums, seg_all, valid_all):
    length, head_local, head_width = queries.shape
    block_rows = min(512, length)
    block_count = length // block_rows
    score_scale = float(head_width) ** (-0.5)
    row_ids = jnp.arange(length, dtype=jnp.int32).reshape(block_count, block_rows)

    def one_block(carried, block_items):
        key_grad, value_grad = carried
        query_block, grad_block, lse_block, seg_block, row_block = block_items
        scores = (
            jnp.einsum("qhd,khd->hqk", query_block, key_heads, preferred_element_type=jnp.float32)
            * score_scale
        )
        allowed = allowed_mask(seg_block, row_block, seg_all, valid_all)[None]
        scores = jnp.where(allowed, scores, -1e30)
        weights = jnp.exp(scores - lse_block[..., None])
        weights_low = weights.astype(jnp.bfloat16)
        value_grad = value_grad + jnp.einsum(
            "hqk,qhd->khd", weights_low, grad_block, preferred_element_type=jnp.float32
        )
        weight_grad = jnp.einsum(
            "qhd,khd->hqk", grad_block, value_heads, preferred_element_type=jnp.float32
        )
        inner_sum = jnp.sum(weights * weight_grad, axis=-1, keepdims=True)
        score_grad = (weights * (weight_grad - inner_sum)).astype(jnp.bfloat16)
        query_grad = (
            jnp.einsum("hqk,khd->qhd", score_grad, key_heads, preferred_element_type=jnp.float32)
            * score_scale
        )
        key_grad = (
            key_grad
            + jnp.einsum(
                "hqk,qhd->khd", score_grad, query_block, preferred_element_type=jnp.float32
            )
            * score_scale
        )
        return ((key_grad, value_grad), query_grad)

    empty_grad = jnp.zeros((length, head_local, head_width), jnp.float32)
    block_items = (
        queries.reshape(block_count, block_rows, head_local, head_width),
        grad_out.reshape(block_count, block_rows, head_local, head_width),
        log_sums,
        seg_all.reshape(block_count, block_rows),
        row_ids,
    )
    (key_grad, value_grad), query_grads = lax.scan(one_block, (empty_grad, empty_grad), block_items)
    return (query_grads.reshape(length, head_local, head_width), key_grad, value_grad)


def on_device(
    hidden_in,
    segment_ids,
    valid_tokens,
    w_qkv,
    w_attn_out,
    w_in_proj,
    w_out_proj,
    attn_gain,
    mlp_gain,
    cotangent,
):
    seq_size = lax.axis_size("seq")
    seq_index = lax.axis_index("seq")
    inputs = hidden_in[0].astype(jnp.float32)
    tokens = inputs.shape[0]
    length = tokens * seq_size
    head_local = HEADS // seq_size
    seg_all = segment_ids[0]
    valid_all = valid_tokens[0]
    offset = seq_index * tokens
    valid_mine = lax.dynamic_slice_in_dim(valid_all, offset, tokens).astype(jnp.float32)[:, None]
    positions = offset + jnp.arange(tokens, dtype=jnp.int32)
    attn_full = (
        lax.all_gather(w_qkv, "fsdp", axis=0, tiled=True),
        lax.all_gather(w_attn_out, "fsdp", axis=0, tiled=True),
        lax.all_gather(attn_gain, "fsdp", axis=0, tiled=True),
    )
    mlp_full = (
        lax.all_gather(w_in_proj, "fsdp", axis=0, tiled=True),
        lax.all_gather(w_out_proj, "fsdp", axis=0, tiled=True),
        lax.all_gather(mlp_gain, "fsdp", axis=0, tiled=True),
    )
    qkv_weight, out_weight, gain_one = attn_full
    in_weight, down_weight, gain_two = mlp_full
    gain_one = gain_one.astype(jnp.float32)
    gain_two = gain_two.astype(jnp.float32)
    normed_low = norm_rows(inputs, gain_one).astype(jnp.bfloat16)
    projected = jnp.dot(normed_low, qkv_weight, preferred_element_type=jnp.float32).reshape(
        tokens, 3, HEADS, HD
    )

    def rope_pair(pair_heads):
        return jnp.stack(
            [rotate(pair_heads[:, 0], positions), rotate(pair_heads[:, 1], positions)], axis=1
        )

    turned = jnp.concatenate([rope_pair(projected[:, :2]), projected[:, 2:]], axis=1).astype(
        jnp.bfloat16
    )
    by_heads = lax.all_to_all(
        turned.reshape(tokens, 3, seq_size, head_local * HD),
        "seq",
        split_axis=2,
        concat_axis=0,
        tiled=True,
    )
    by_heads = by_heads.reshape(length, 3, head_local, HD)
    queries = by_heads[:, 0]
    key_heads = by_heads[:, 1]
    value_heads = by_heads[:, 2]
    attended, log_sums = attend_forward(queries, key_heads, value_heads, seg_all, valid_all)
    attended_low = attended.astype(jnp.bfloat16).reshape(length, 1, head_local * HD)
    mixed_low = lax.all_to_all(
        attended_low, "seq", split_axis=0, concat_axis=1, tiled=True
    ).reshape(tokens, D)
    attn_branch = jnp.dot(mixed_low, out_weight, preferred_element_type=jnp.float32)
    middle = inputs + attn_branch
    normed_two_low = norm_rows(middle, gain_two).astype(jnp.bfloat16)
    widened = jnp.dot(normed_two_low, in_weight, preferred_element_type=jnp.float32)
    inner_in = widened[:, :FF]
    inner_gate = widened[:, FF:]
    hidden_low = gelu_gate(inner_in, inner_gate).astype(jnp.bfloat16)
    mlp_branch = jnp.dot(hidden_low, down_weight, preferred_element_type=jnp.float32)
    result = middle + mlp_branch
    stat_sums = lax.psum(
        (
            jnp.sum(valid_mine * result * result),
            jnp.sum(valid_mine * attn_branch * attn_branch),
            jnp.sum(valid_mine * mlp_branch * mlp_branch),
            jnp.sum(valid_mine),
        ),
        ("seq", "fsdp"),
    )
    valid_count = jnp.maximum(stat_sums[3], 1.0)
    root_means = jnp.sqrt(jnp.stack([stat_sums[0], stat_sums[1], stat_sums[2]]) / (valid_count * D))
    back_attn = (
        lax.all_gather(w_qkv, "fsdp", axis=0, tiled=True),
        lax.all_gather(w_attn_out, "fsdp", axis=0, tiled=True),
        lax.all_gather(attn_gain, "fsdp", axis=0, tiled=True),
    )
    back_mlp = (
        lax.all_gather(w_in_proj, "fsdp", axis=0, tiled=True),
        lax.all_gather(w_out_proj, "fsdp", axis=0, tiled=True),
        lax.all_gather(mlp_gain, "fsdp", axis=0, tiled=True),
    )
    qkv_back, out_back = (back_attn[0], back_attn[1])
    in_back, down_back = (back_mlp[0], back_mlp[1])
    grad_result = cotangent[0].astype(jnp.float32)
    grad_mlp_low = grad_result.astype(jnp.bfloat16)
    grad_down = jnp.einsum(
        "tf,td->fd", hidden_low, grad_mlp_low, preferred_element_type=jnp.float32
    )
    grad_hidden = jnp.einsum(
        "td,fd->tf", grad_mlp_low, down_back, preferred_element_type=jnp.float32
    )
    _, gelu_pull = jax.vjp(gelu_gate, inner_in, inner_gate)
    grad_inner_in, grad_inner_gate = gelu_pull(grad_hidden)
    grad_widened = jnp.concatenate([grad_inner_in, grad_inner_gate], axis=1).astype(jnp.bfloat16)
    grad_in_weight = jnp.einsum(
        "td,tf->df", normed_two_low, grad_widened, preferred_element_type=jnp.float32
    )
    grad_normed_two = jnp.einsum(
        "tf,df->td", grad_widened, in_back, preferred_element_type=jnp.float32
    )
    _, second_pull = jax.vjp(norm_rows, middle, gain_two)
    grad_middle_part, grad_gain_two = second_pull(grad_normed_two)
    grad_middle = grad_result + grad_middle_part
    mlp_sums = (
        lax.psum_scatter(grad_in_weight, "fsdp", scatter_dimension=0, tiled=True),
        lax.psum_scatter(grad_down, "fsdp", scatter_dimension=0, tiled=True),
        lax.psum_scatter(grad_gain_two, "fsdp", scatter_dimension=0, tiled=True),
    )
    grad_attn_low = grad_middle.astype(jnp.bfloat16)
    grad_out_weight = jnp.einsum(
        "td,te->de", mixed_low, grad_attn_low, preferred_element_type=jnp.float32
    )
    grad_mixed = jnp.einsum(
        "te,de->td", grad_attn_low, out_back, preferred_element_type=jnp.float32
    ).astype(jnp.bfloat16)
    grad_by_heads = lax.all_to_all(
        grad_mixed.reshape(tokens, seq_size, head_local * HD),
        "seq",
        split_axis=1,
        concat_axis=0,
        tiled=True,
    )
    grad_by_heads = grad_by_heads.reshape(length, head_local, HD)
    query_grad, key_grad, value_grad = attend_backward(
        queries, key_heads, value_heads, grad_by_heads, log_sums, seg_all, valid_all
    )
    stacked = (
        jnp.stack([query_grad, key_grad, value_grad], axis=1)
        .astype(jnp.bfloat16)
        .reshape(length, 3, 1, head_local * HD)
    )
    grad_turned = (
        lax.all_to_all(stacked, "seq", split_axis=0, concat_axis=2, tiled=True)
        .reshape(tokens, 3, HEADS, HD)
        .astype(jnp.float32)
    )
    _, rope_pull = jax.vjp(rope_pair, projected[:, :2])
    (grad_pair,) = rope_pull(grad_turned[:, :2])
    grad_projected = (
        jnp.concatenate([grad_pair, grad_turned[:, 2:]], axis=1)
        .reshape(tokens, 3 * D)
        .astype(jnp.bfloat16)
    )
    grad_qkv_weight = jnp.einsum(
        "td,te->de", normed_low, grad_projected, preferred_element_type=jnp.float32
    )
    grad_normed = jnp.einsum(
        "te,de->td", grad_projected, qkv_back, preferred_element_type=jnp.float32
    )
    _, first_pull = jax.vjp(norm_rows, inputs, gain_one)
    grad_input_part, grad_gain_one = first_pull(grad_normed)
    grad_inputs = grad_middle + grad_input_part
    attn_sums = (
        lax.psum_scatter(grad_qkv_weight, "fsdp", scatter_dimension=0, tiled=True),
        lax.psum_scatter(grad_out_weight, "fsdp", scatter_dimension=0, tiled=True),
        lax.psum_scatter(grad_gain_one, "fsdp", scatter_dimension=0, tiled=True),
    )
    summed = lax.psum(
        (attn_sums[0], attn_sums[1], attn_sums[2], mlp_sums[0], mlp_sums[1], mlp_sums[2]), "seq"
    )
    final_grads = (summed[0], summed[1], summed[3], summed[4], summed[2], summed[5])
    return (
        result.astype(jnp.bfloat16)[None],
        grad_inputs[None],
        final_grads[0],
        final_grads[1],
        final_grads[2],
        final_grads[3],
        final_grads[4],
        final_grads[5],
        root_means,
    )


def solution(mesh):
    in_specs = (
        P("fsdp", "seq", None),
        P("fsdp", None),
        P("fsdp", None),
        P("fsdp", None),
        P("fsdp", None),
        P("fsdp", None),
        P("fsdp", None),
        P("fsdp"),
        P("fsdp"),
        P("fsdp", "seq", None),
    )
    out_specs = (
        P("fsdp", "seq", None),
        P("fsdp", "seq", None),
        P("fsdp", None),
        P("fsdp", None),
        P("fsdp", None),
        P("fsdp", None),
        P("fsdp"),
        P("fsdp"),
        P(),
    )
    return jax.shard_map(
        on_device, mesh=mesh, in_specs=in_specs, out_specs=out_specs, check_vma=False
    )
```

profile of v0, /device:TPU:0, one launch (start us, length us, event | category | flops | bytes accessed | tf_op | source)
XLA Modules:
  0.0 950.7 jit_solution(4761089183071408924)
XLA Ops:
  9.4 13.6 %all-gather = bf16[8,1,128]{2,1,0:T(2,128)(2,1)S(1)} all-gather(bf16[1,1,128]{2,1,0:T(2,128)(2,1)} %bitcast.267), channel_id=1, replica_groups=mesh['seq'=4,'fsdp'=8] {'fsdp'}, dimensions={0}, use_global_device_ids=true | all-gather | bytes 2304 | tf_op jit(solution)/shard_map/all_gather | solution.py:160
  24.8 52.3 %all-gather.7.cloned.1.call-done = bf16[1024,3072]{1,0:T(8,128)(2,1)} async-done(((bf16[128,3072]{1,0:T(8,128)(2,1)}), bf16[1024,3072]{1,0:T(8,128)(2,1)}) %all-gather.7.cloned.1.call-update) | async-done | bytes 6291472 | tf_op jit(solution)/shard_map/all_gather | solution.py:158
  77.1 8.7 copy.74
  85.8 4.8 fusion.65
  92.7 3.6 all-to-all-start
  98.1 18.0 %all-to-all-done = bf16[256,3,4,256]{0,3,1,2:T(8,128)(2,1)S(1)} async-done(((bf16[256,3,4,256]{0,3,1,2:T(8,128)(2,1)}), bf16[256,3,4,256]{0,3,1,2:T(8,128)(2,1)S(1)}, u32[]{:S(2)}, u32[]{:S(2)}) %all-to-all-start) | async-done | bytes 1572896 | tf_op jit(solution)/shard_map/all_to_all | solution.py:184
  116.2 2.4 copy.78
  118.6 3.8 reshape.478
  124.5 15.6 %while.27 = (s32[]{:T(128)}, bf16[2,512,4,64]{1,3,2,0:T(8,128)(2,1)S(1)}, f32[2,4,512]{2,1,0:T(4,128)S(1)}, s32[2,512]{1,0:T(2,128)S(1)}, s32[1,1024]{1,0:T(1,12...) while((s32[]{:T(128)}, ...), condition=%wide.region_5.6_spmd, body=%wide.region_2.5_spmd.sunk | while | flops 564132864 | bytes 29186172 | solution.py:72
  125.2 1.7 fusion.133
  126.9 2.3 fusion.134
  129.2 3.0 fusion.135
  133.0 1.7 fusion.133
  134.7 2.3 fusion.134
  137.1 3.0 fusion.135
  141.5 3.9 reshape.490
  146.0 4.6 reduce.10
  150.6 2.0 reshape.507
  152.6 4.1 all-to-all-start.1
  156.8 10.5 %all-gather.1 = bf16[8,1,128]{2,1,0:T(2,128)(2,1)S(1)} all-gather(bf16[1,1,128]{2,1,0:T(2,128)(2,1)S(1)} %bitcast.268), channel_id=1, replica_groups=mesh['seq'=4,'fsdp'=8] {'fsdp'}, dimensions={0}, use_global_device_ids=true | all-gather | bytes 2304 | tf_op jit(solution)/shard_map/all_gather | solution.py:165
  167.9 2.2 reshape.508
  171.0 2.0 copy.82
  173.0 3.5 fusion.84
  176.8 32.4 %all-gather.11.cloned.1.call-done = bf16[1024,5248]{1,0:T(8,128)(2,1)} async-done(((bf16[128,5248]{1,0:T(8,128)(2,1)}), bf16[1024,5248]{1,0:T(8,128)(2,1)}) %all-gather.11.cloned.1.call-update) | async-done | bytes 10747920 | tf_op jit(solution)/shard_map/all_gather | solution.py:163
  209.2 9.0 fusion.81
  218.2 47.9 %all-gather.13.cloned.1.call-done = bf16[2624,1024]{1,0:T(8,128)(2,1)} async-done(((bf16[328,1024]{1,0:T(8,128)(2,1)}), bf16[2624,1024]{1,0:T(8,128)(2,1)}) %all-gather.13.cloned.1.call-update) | async-done | bytes 5373968 | tf_op jit(solution)/shard_map/all_gather | solution.py:164
  266.1 9.1 add_convert_fusion
  275.2 6.3 fusion.47
  281.5 6.7 fusion.61
  289.8 2.8 fusion.86
  293.7 7.0 fusion.67
  300.7 2.3 convolution_convert_fusion
  304.0 3.6 all-to-all-start.2
  307.9 8.3 all-to-all-done.2
  317.4 1.9 reshape_reshape.3
  321.0 42.2 %while.28 = (s32[]{:T(128)}, f32[1024,4,64]{0,2,1:T(8,128)S(1)}, f32[1024,4,64]{0,2,1:T(8,128)}, bf16[2,512,4,64]{1,3,2,0:T(8,128)(2,1)}, bf16[2,512,4,64]{1,3,2...) while((s32[]{:T(128)}, f32[1024,4,64]{0,2,1:T(8,128)S(1)}, ...), condition=%wide.region_12.13_spmd.clone, body=%wide.region_10.12_spmd.clone.sunk | while | flops 1377172480 | bytes 143735600 | solution.py:130
  323.1 3.2 multiply_reduce_fusion.5
  326.3 3.7 multiply_convert_fusion.7
  330.0 3.3 fusion.147
  333.3 4.8 fusion.149
  338.1 3.6 fusion.148
  343.7 3.2 multiply_reduce_fusion.5
  346.9 3.7 multiply_convert_fusion.7
  350.6 3.3 fusion.147
  353.9 4.7 fusion.149
  358.6 4.6 fusion.148
  367.8 2.9 copy.90
  370.8 28.0 %all_to_all.54 = bf16[1024,3,1,256]{3,1,2,0:T(4,128)(2,1)S(1)} all-to-all(bf16[1024,3,1,256]{3,1,2,0:T(4,128)(2,1)S(1)} %copy.90), channel_id=1, replica_groups=mesh['seq'=4,'fsdp'=8] {'seq'}, dimensions={0} | all-to-all | bytes 3145728 | tf_op jit(solution)/shard_map/all_to_all | solution.py:281
  399.3 2.3 copy.92
  403.0 1.8 slice_bitcast_fusion.1
  406.4 6.6 fusion.71
  414.2 11.0 %fusion.46 = f32[1024,5248]{1,0:T(8,128)} fusion(bf16[256,2624]{1,0:T(8,128)(2,1)} %get-tuple-element.352, bf16[256,2624]{1,0:T(8,128)(2,1)} %get-tuple-element.351, f32[256,1024]{1,0:T(8,128)S(1)} %copy-done.3, f32[1024]{0:T(1024)S(1)} %bitcast.254, f32[256]{0:T(256)S(1)} %fusion.74, f32[256]{0:T(256)S(1)} %broadcast_multiply_fusion), kind=kOutput, calls=%fused_computation.69 | convolution fusion | flops 2757885952 | bytes 25237504 | tf_op jit(solution)/shard_map/td,tf->df/dot_general | solution.py:243
  425.3 28.7 %reduce-scatter.11.cloned.1.call-done = f32[328,1024]{1,0:T(8,128)} async-done(((f32[2624,1024]{1,0:T(8,128)}), f32[328,1024]{1,0:T(8,128)}) %reduce-scatter.11.cloned.1.call-update) | async-done | bytes 1343504 | tf_op jit(solution)/shard_map/reduce_scatter | solution.py:254
  454.0 129.9 %reduce-scatter.5.cloned.1.call-done = f32[128,3072]{1,0:T(8,128)} async-done(((f32[1024,3072]{1,0:T(8,128)}), f32[128,3072]{1,0:T(8,128)}) %reduce-scatter.5.cloned.1.call-update) | async-done | bytes 1572880 | tf_op jit(solution)/shard_map/reduce_scatter | solution.py:302
  583.9 213.4 %reduce-scatter.9.cloned.1.call-done = f32[128,5248]{1,0:T(8,128)} async-done(((f32[1024,5248]{1,0:T(8,128)}), f32[128,5248]{1,0:T(8,128)}) %reduce-scatter.9.cloned.1.call-update) | async-done | bytes 2686992 | tf_op jit(solution)/shard_map/reduce_scatter | solution.py:253
  798.6 39.2 %all-reduce.8 = (f32[1]{0:T(128)}, f32[1]{0:T(128)}, f32[1]{0:T(128)}, f32[]{:T(128)}) all-reduce(f32[1]{0:T(128)} %bitcast.50, f32[1]{0:T(128)} %bitcast.49, f32[1]{0:T(128)} %bitcast.48, f32[]{:T(128)} %get-tuple-element.337), channel_id=1, replica_groups=mesh['seq'=4,'fsdp'=8] {'seq','fsdp'}, use_global_device_ids=true, to_apply=%region_34.35 | all-reduce | flops 4 | bytes 32 | tf_op jit(solution)/shard_map/psum | solution.py:209
  838.4 2.5 fusion.75
  841.0 5.0 fusion.55
  847.5 16.0 %all-reduce.9 = (f32[1024]{0:T(1024)S(1)}, f32[1024]{0:T(1024)S(1)}) all-reduce(f32[1024]{0:T(1024)S(1)} %get-tuple-element.272, f32[1024]{0:T(1024)S(1)} %copy-done.36), channel_id=6, replica_groups=mesh['seq'=4,'fsdp'=8] {'fsdp'}, use_global_device_ids=true, to_apply=%region_24.25.clone | all-reduce | flops 2048 | bytes 16384
  863.6 9.2 all-reduce.10
  872.8 2.9 add_bitcast_fusion
  875.7 60.8 %all-reduce.14.cloned.1.call-done = (f32[128,3072]{1,0:T(8,128)}, f32[128,1024]{1,0:T(8,128)}, f32[128,5248]{1,0:T(8,128)}, f32[328,1024]{1,0:T(8,128)}) async-done(((f32[128,3072]{1,0:T(8,128)}, f32[128,1024]{1,0:T(8,128)}, f32[128,5248]{1,0:T(8,128)}, f32[328,1024]{1,0:T(8,128)}), (f32[128,3072]{1,0:T(8,128)}, f32[128,1024]{1,0:T(8,128)}, f32[128,5248]{1,0:T(8,128)}, ...) | async-done | bytes 6127632 | tf_op jit(solution)/shard_map/psum | solution.py:306
  936.5 2.9 copy.127
  939.4 2.0 copy.128
  (186 shorter events, 39.9 us)
Async XLA Ops:
  7.2 17.1 %copy-start.4 = (bf16[1,256,1024]{2,1,0:T(8,128)(2,1)S(1)}, bf16[1,256,1024]{2,1,0:T(8,128)(2,1)}, u32[]{:S(2)}) copy-start(bf16[1,256,1024]{2,1,0:T(8,128)(2,1)} %param.14) | copy-start | bytes 1572868
  7.2 69.9 %all-gather.7.cloned.1.call-start = ((), (), s32[]{:S(2)}) async-start(), calls=%async_computation.8 | async-start | bytes 7077888 | tf_op jit(solution)/shard_map/all_gather | solution.py:158
  7.9 165.1 %all-gather.9.cloned.1.call-start = ((), (), s32[]{:S(2)}) async-start(), calls=%async_computation.9 | async-start | bytes 2359296 | tf_op jit(solution)/shard_map/all_gather | solution.py:159
  8.7 200.5 %all-gather.11.cloned.1.call-start = ((), (), s32[]{:S(2)}) async-start(), calls=%async_computation.10 | async-start | bytes 12091392 | tf_op jit(solution)/shard_map/all_gather | solution.py:163
  23.0 62.7 %copy-start.26 = (f32[8,1,128]{2,1,0:T(1,128)}, f32[8,1,128]{2,1,0:T(1,128)S(1)}, u32[]{:S(2)}) copy-start(f32[8,1,128]{2,1,0:T(1,128)S(1)} %convert_element_type.149) | copy-start | bytes 12292
  24.3 61.5 %copy-start.28 = (f32[256]{0:T(256)}, f32[256]{0:T(256)S(1)}, u32[]{:S(2)}) copy-start(f32[256]{0:T(256)S(1)} %broadcast_multiply_fusion.1) | copy-start | bytes 3076
  24.6 61.2 %copy-start.34 = (f32[256]{0:T(256)}, f32[256]{0:T(256)S(1)}, u32[]{:S(2)}) copy-start(f32[256]{0:T(256)S(1)} %fusion.54) | copy-start | bytes 3076
  24.6 61.2 %copy-start.30 = (f32[256]{0:T(256)}, f32[256]{0:T(256)S(1)}, u32[]{:S(2)}) copy-start(f32[256]{0:T(256)S(1)} %fusion.73) | copy-start | bytes 3076
  24.8 66.1 %copy-start.22 = (f32[256,32]{0,1:T(8,128)}, f32[256,32]{0,1:T(8,128)S(1)}, u32[]{:S(2)}) copy-start(f32[256,32]{0,1:T(8,128)S(1)} %get-tuple-element.374) | copy-start | bytes 98308
  24.8 66.1 %copy-start.24 = (f32[256,32]{0,1:T(8,128)}, f32[256,32]{0,1:T(8,128)S(1)}, u32[]{:S(2)}) copy-start(f32[256,32]{0,1:T(8,128)S(1)} %get-tuple-element.375) | copy-start | bytes 98308
  91.4 6.1 copy-start.20
  92.7 23.5 %all-to-all-start = ((bf16[256,3,4,256]{0,3,1,2:T(8,128)(2,1)}), bf16[256,3,4,256]{0,3,1,2:T(8,128)(2,1)S(1)}, u32[]{:S(2)}, u32[]{:S(2)}) async-start(bf16[256,3,4,256]{0,3,1,2:T(8,128)(2,1)} %pad_maximum_fusion.3), calls=%async_computation | async-start | bytes 3145728 | tf_op jit(solution)/shard_map/all_to_all | solution.py:184
  96.4 169.7 %all-gather.13.cloned.1.call-start = ((), (), s32[]{:S(2)}) async-start(), calls=%async_computation.11 | async-start | bytes 6045696 | tf_op jit(solution)/shard_map/all_gather | solution.py:164
  122.4 2.1 copy-start.21
  141.5 15.3 %copy-start.37 = (bf16[128]{0:T(256)(128)(2,1)S(1)}, bf16[128]{0:T(256)(128)(2,1)}, u32[]{:S(2)}) copy-start(bf16[128]{0:T(256)(128)(2,1)} %param.22) | copy-start | bytes 772
  152.6 15.3 %all-to-all-start.1 = ((bf16[4,2,32768]{2,1,0:T(2,128)(2,1)}), bf16[4,2,32768]{2,1,0:T(2,128)(2,1)}, u32[]{:S(2)}, u32[]{:S(2)}) async-start(bf16[4,2,32768]{2,1,0:T(2,128)(2,1)} %reshape.507), calls=%async_computation.1 | async-start | bytes 1048576 | tf_op jit(solution)/shard_map/all_to_all | solution.py:197
  156.7 268.6 %reduce-scatter.7.cloned.1.call-start = ((), (), s32[]{:S(2)}) async-start(), calls=%async_computation.13 | async-start | bytes 4718592 | tf_op jit(solution)/shard_map/reduce_scatter | solution.py:303
  176.5 111.7 %copy-start.2 = (f32[256,1024]{1,0:T(8,128)}, f32[256,1024]{1,0:T(8,128)S(1)}, u32[]{:S(2)}) copy-start(f32[256,1024]{1,0:T(8,128)S(1)} %get-tuple-element.342) | copy-start | bytes 3145732
  209.2 56.9 %copy-start.12 = (bf16[1,256,1024]{2,1,0:T(8,128)(2,1)S(1)}, bf16[1,256,1024]{2,1,0:T(8,128)(2,1)}, u32[]{:S(2)}) copy-start(bf16[1,256,1024]{2,1,0:T(8,128)(2,1)} %param.23) | copy-start | bytes 1572868
  266.1 9.1 copy-start.6
  275.2 6.3 copy-start.17
  281.5 6.8 copy-start.19
  288.2 1.4 copy-start.13
  288.2 1.6 copy-start.9
  288.7 1.0 copy-start.7
  288.7 4.0 copy-start.32
  292.6 1.0 copy-start.14
  292.7 161.3 %reduce-scatter.11.cloned.1.call-start = ((), (), s32[]{:S(2)}) async-start(), calls=%async_computation.15 | async-start | bytes 12091392 | tf_op jit(solution)/shard_map/reduce_scatter | solution.py:254
  304.0 12.2 %all-to-all-start.2 = ((bf16[256,4,256]{0,2,1:T(8,128)(2,1)}), bf16[256,4,256]{0,2,1:T(8,128)(2,1)S(1)}, u32[]{:S(2)}, u32[]{:S(2)}) async-start(bf16[256,4,256]{0,2,1:T(8,128)(2,1)} %bitcast.33), calls=%async_computation.2 | async-start | bytes 1048576 | tf_op jit(solution)/shard_map/all_to_all | solution.py:264
  307.7 276.2 %reduce-scatter.5.cloned.1.call-start = ((), (), s32[]{:S(2)}) async-start(), calls=%async_computation.12 | async-start | bytes 14155776 | tf_op jit(solution)/shard_map/reduce_scatter | solution.py:302
  321.7 1.3 copy-start.10
  323.0 3.2 copy-start
  330.0 8.2 copy-start.1
  333.3 4.8 copy-start.11
  342.4 1.3 copy-start.10
  343.7 3.2 copy-start
  350.6 8.0 copy-start.1
  353.9 4.7 copy-start.11
  401.7 3.1 copy-start.23
  401.7 3.1 copy-start.25
  405.4 1.0 copy-start.5
  405.4 1.0 copy-start.27
  405.4 1.0 copy-start.29
  405.4 1.0 copy-start.31
  413.0 1.2 copy-start.3
  413.0 384.3 %reduce-scatter.9.cloned.1.call-start = ((), (), s32[]{:S(2)}) async-start(), calls=%async_computation.14 | async-start | bytes 24182784 | tf_op jit(solution)/shard_map/reduce_scatter | solution.py:253
  425.2 372.1 %copy-start.38 = (u32[32]{0:T(128)S(1)}, u32[32]{0:T(128)}, u32[]{:S(2)}) copy-start(u32[32]{0:T(128)} %constant.113) | copy-start | bytes 388
  425.2 511.3 %all-reduce.14.cloned.1.call-start = ((), (), s32[]{:S(2)}) async-start(), calls=%async_computation.16 | async-start | bytes 12255232 | tf_op jit(solution)/shard_map/psum | solution.py:306
  840.9 5.0 copy-start.35
  840.9 6.5 copy-start.36
  841.0 31.9 %copy-start.8 = (f32[256,1024]{1,0:T(8,128)S(1)}, f32[256,1024]{1,0:T(8,128)}, u32[]{:S(2)}) copy-start(f32[256,1024]{1,0:T(8,128)} %copy-done.7) | copy-start | bytes 3145732
  841.0 31.9 %copy-start.33 = (f32[256]{0:T(256)S(1)}, f32[256]{0:T(256)}, u32[]{:S(2)}) copy-start(f32[256]{0:T(256)} %copy-done.32) | copy-start | bytes 3076
  845.9 1.0 copy-start.15
  936.5 4.8 copy-start.16
  939.4 3.5 copy-start.18
Sparse Core Ops, SparseCore 0:
  9.6 67.4 all-gather.6
  78.7 27.8 all-gather.8
  108.2 100.9 all-gather.10
  210.7 55.3 all-gather.12
  292.8 48.6 reduce-scatter.6
  343.7 110.2 reduce-scatter.10
  456.3 127.5 reduce-scatter.4
  586.3 210.9 reduce-scatter.8
  801.2 135.2 all-reduce.13
where the time goes:
time: 956 us; the launch traced here: 951 us
  waiting for transfers between devices  594 us (62%)
  matrix products  117 us (12%)
  blocking collectives  116 us (12%)
  local copies, waits for them, and re-layouts  60.1 us (6%)
  other arithmetic  34.9 us (4%)
  between operations  16 us (2%)
  starting transfers between devices  12.1 us (1%)
    reduce_scatter x1, waiting for transfers between devices, on_device(): lax.psum_scatter(grad_in_weight, 'fsdp', scatter_dimension=0, tiled=True)  213 us
    reduce_scatter x1, waiting for transfers between devices, on_device(): lax.psum_scatter(grad_qkv_weight, 'fsdp', scatter_dimension=0, tiled=True)  130 us
    psum x1, waiting for transfers between devices, on_device(): lax.psum((attn_sums[0], attn_sums[1], attn_sums[2], mlp_sums[0], mlp_sums...  60.8 us
    all_gather x1, waiting for transfers between devices, on_device(): lax.all_gather(w_qkv, 'fsdp', axis=0, tiled=True)  52.3 us
    all_gather x1, waiting for transfers between devices, on_device(): lax.all_gather(w_out_proj, 'fsdp', axis=0, tiled=True)  47.9 us
    psum x1, blocking collectives, on_device(): lax.psum((jnp.sum(valid_mine * result * result), jnp.sum(valid_mine * att...  39.2 us
    all_gather x1, waiting for transfers between devices, on_device(): lax.all_gather(w_in_proj, 'fsdp', axis=0, tiled=True)  32.4 us
    reduce_scatter x1, waiting for transfers between devices, on_device(): lax.psum_scatter(grad_down, 'fsdp', scatter_dimension=0, tiled=True)  28.7 us
  transfers between devices with their start and end apart: 12, of which 9 were waited for; matrix products, arithmetic and copies ran while one was open for 18% of the time, Pallas kernels for 0%

commit v1 on v0

--- a/solution.py
+++ b/solution.py
@@ -9,6 +9,18 @@
 FF = 2624
 ROPE_BASE = 160000.0
 NORM_EPS = 1e-05
+
+
+def gather_by_bits(x, axis, dim):
+    ways, here = (lax.axis_size(axis), lax.axis_index(axis))
+    grown, reach = (x, 1)
+    while reach < ways:
+        theirs = lax.ppermute(grown, axis, [(d, d ^ reach) for d in range(ways)])
+        mine_first = jnp.concatenate([grown, theirs], axis=dim)
+        theirs_first = jnp.concatenate([theirs, grown], axis=dim)
+        grown = jnp.where(here & reach == 0, mine_first, theirs_first)
+        reach = 2 * reach
+    return grown
 
 
 def norm_rows(values, gain_row):
@@ -160,7 +172,7 @@
         lax.all_gather(attn_gain, "fsdp", axis=0, tiled=True),
     )
     mlp_full = (
-        lax.all_gather(w_in_proj, "fsdp", axis=0, tiled=True),
+        gather_by_bits(w_in_proj, "fsdp", 0),
         lax.all_gather(w_out_proj, "fsdp", axis=0, tiled=True),
         lax.all_gather(mlp_gain, "fsdp", axis=0, tiled=True),
     )

time: 956 us -> 1220 us (1.28)
  waiting for transfers between devices: 594 us -> 750 us
  blocking collectives: 116 us -> 209 us
    ppermute x0 -> x3, waiting for transfers between devices: none -> 205 us  [gather_by_bits(): theirs = lax.ppermute(grown, axis, [(d, d ^ reach) for d in range(ways)])]
    all_gather x1, blocking collectives: 10.5 us -> 104 us  [on_device(): lax.all_gather(mlp_gain, 'fsdp', axis=0, tiled=True)]
    all_gather x1, waiting for transfers between devices: 47.9 us -> 0.01 us  [on_device(): lax.all_gather(w_out_proj, 'fsdp', axis=0, tiled=True)]
    all_gather x1, waiting for transfers between devices: 52.3 us -> 87.9 us  [on_device(): lax.all_gather(w_qkv, 'fsdp', axis=0, tiled=True)]
    all_gather x1, waiting for transfers between devices: 32.4 us -> 0.01 us  [on_device(): lax.all_gather(w_in_proj, 'fsdp', axis=0, tiled=True)]
    all_to_all x1, waiting for transfers between devices: 18 us -> 1.3 us  [on_device(): lax.all_to_all(turned.reshape(tokens, 3, seq_size, head_local * HD), 'seq...]
    reduce_scatter x1, waiting for transfers between devices: 28.7 us -> 42.1 us  [on_device(): lax.psum_scatter(grad_down, 'fsdp', scatter_dimension=0, tiled=True)]
  transfers between devices with their start and end apart: 12 -> 15, of which waited for: 9 -> 8; matrix products, arithmetic and copies ran while one was open for 18% -> 16% of each run, Pallas kernels for 0% -> 0%
where the time goes in v1:
time: 1220 us
  waiting for transfers between devices  750 us (61%)
  blocking collectives  209 us (17%)
  matrix products  116 us (10%)
  local copies, waits for them, and re-layouts  60.3 us (5%)
  other arithmetic  44.6 us (4%)
  starting transfers between devices  22 us (2%)
  between operations  16 us (1%)
    reduce_scatter x1, waiting for transfers between devices, on_device(): lax.psum_scatter(grad_in_weight, 'fsdp', scatter_dimension=0, tiled=True)  213 us
    ppermute x3, waiting for transfers between devices, gather_by_bits(): theirs = lax.ppermute(grown, axis, [(d, d ^ reach) for d in range(ways)])  205 us
    reduce_scatter x1, waiting for transfers between devices, on_device(): lax.psum_scatter(grad_qkv_weight, 'fsdp', scatter_dimension=0, tiled=True)  130 us
    all_gather x1, blocking collectives, on_device(): lax.all_gather(mlp_gain, 'fsdp', axis=0, tiled=True)  104 us
    all_gather x1, waiting for transfers between devices, on_device(): lax.all_gather(w_qkv, 'fsdp', axis=0, tiled=True)  87.9 us
    psum x1, waiting for transfers between devices, on_device(): lax.psum((attn_sums[0], attn_sums[1], attn_sums[2], mlp_sums[0], mlp_sums...  60.8 us
    reduce_scatter x1, waiting for transfers between devices, on_device(): lax.psum_scatter(grad_down, 'fsdp', scatter_dimension=0, tiled=True)  42.1 us
    psum x1, blocking collectives, on_device(): lax.psum((jnp.sum(valid_mine * result * result), jnp.sum(valid_mine * att...  39.2 us
  transfers between devices with their start and end apart: 15, of which 8 were waited for; matrix products, arithmetic and copies ran while one was open for 16% of the time, Pallas kernels for 0%

profile of v1, /device:TPU:0, one launch (start us, length us, event | category | flops | bytes accessed | tf_op | source)
XLA Modules:
  0.0 1218.8 jit_solution(4594216629439415807)
XLA Ops:
  10.6 13.2 %all-gather = bf16[8,1,128]{2,1,0:T(2,128)(2,1)S(1)} all-gather(bf16[1,1,128]{2,1,0:T(2,128)(2,1)} %bitcast.266), channel_id=1, replica_groups=mesh['seq'=4,'fsdp'=8] {'fsdp'}, dimensions={0}, use_global_device_ids=true | all-gather | bytes 2304 | tf_op jit(solution)/shard_map/all_gather | solution.py:172
  24.9 1.9 maximum_select_fusion.3
  27.4 87.9 %all-gather.7.cloned.1.call-done = bf16[1024,3072]{1,0:T(8,128)(2,1)} async-done(((bf16[128,3072]{1,0:T(8,128)(2,1)}), bf16[1024,3072]{1,0:T(8,128)(2,1)}) %all-gather.7.cloned.1.call-update) | async-done | bytes 6291472 | tf_op jit(solution)/shard_map/all_gather | solution.py:170
  115.3 8.6 copy.74
  124.0 4.8 fusion.72
  130.9 4.4 all-to-all-start
  136.5 7.8 maximum_select_fusion.2
  144.3 8.3 collective-permute-start.2
  153.9 2.4 copy.78
  156.3 3.8 reshape.478
  160.1 1.7 slice_bitcast_fusion.4
  162.3 15.6 %while.27 = (s32[]{:T(128)}, bf16[2,512,4,64]{1,3,2,0:T(8,128)(2,1)S(1)}, f32[2,4,512]{2,1,0:T(4,128)S(1)}, s32[2,512]{1,0:T(2,128)S(1)}, s32[1,1024]{1,0:T(1,12...) while((s32[]{:T(128)}, ...), condition=%wide.region_5.6_spmd, body=%wide.region_2.5_spmd.sunk | while | flops 564132864 | bytes 29186172 | solution.py:84
  164.8 2.3 fusion.140
  167.1 3.0 fusion.141
  170.9 1.7 fusion.139
  172.6 2.3 fusion.140
  174.9 3.0 fusion.141
  179.4 3.9 reshape.490
  183.8 4.6 reduce.10
  188.4 2.0 reshape.507
  190.4 4.1 all-to-all-start.1
  194.6 104.0 %all-gather.1 = bf16[8,1,128]{2,1,0:T(2,128)(2,1)S(1)} all-gather(bf16[1,1,128]{2,1,0:T(2,128)(2,1)S(1)} %bitcast.267), channel_id=1, replica_groups=mesh['seq'=4,'fsdp'=8] {'fsdp'}, dimensions={0}, use_global_device_ids=true | all-gather | bytes 2304 | tf_op jit(solution)/shard_map/all_gather | solution.py:177
  299.3 2.2 reshape.508
  302.4 2.0 copy.82
  304.4 3.5 fusion.91
  308.2 204.5 %collective-permute-done.2 = bf16[512,5248]{1,0:T(8,128)(2,1)} collective-permute-done((bf16[512,5248]{1,0:T(8,128)(2,1)}, bf16[512,5248]{1,0:T(8,128)(2,1)}, u32[]{:S(2)}, u32[]{:S(2)}) %collective-permute-start.2) | collective-permute-done | bytes 5373984 | tf_op jit(solution)/shard_map/ppermute | solution.py:18
  512.7 10.9 fusion.45
  523.6 9.2 add_convert_fusion
  532.8 6.8 fusion.54
  540.0 3.7 fusion.68
  545.2 2.8 fusion.93
  549.1 7.0 fusion.74
  556.1 2.3 convolution_convert_fusion
  559.4 3.8 all-to-all-start.2
  563.7 7.8 all-to-all-done.2
  572.7 1.9 reshape_reshape.3
  576.3 42.3 %while.28 = (s32[]{:T(128)}, f32[1024,4,64]{0,2,1:T(8,128)S(1)}, f32[1024,4,64]{0,2,1:T(8,128)}, bf16[2,512,4,64]{1,3,2,0:T(8,128)(2,1)}, bf16[2,512,4,64]{1,3,2...) while((s32[]{:T(128)}, f32[1024,4,64]{0,2,1:T(8,128)S(1)}, ...), condition=%wide.region_12.13_spmd.clone, body=%wide.region_10.12_spmd.clone.sunk | while | flops 1377172480 | bytes 143735600 | solution.py:142
  578.3 3.2 multiply_reduce_fusion.5
  581.5 3.7 multiply_convert_fusion.7
  585.2 3.3 fusion.153
  588.6 4.8 fusion.155
  593.4 3.6 fusion.154
  599.0 3.2 multiply_reduce_fusion.5
  602.2 3.7 multiply_convert_fusion.7
  605.9 3.3 fusion.153
  609.3 4.8 fusion.155
  614.0 4.6 fusion.154
  623.3 3.0 copy.90
  626.2 27.5 %all_to_all.54 = bf16[1024,3,1,256]{3,1,2,0:T(4,128)(2,1)S(1)} all-to-all(bf16[1024,3,1,256]{3,1,2,0:T(4,128)(2,1)S(1)} %copy.90), channel_id=1, replica_groups=mesh['seq'=4,'fsdp'=8] {'seq'}, dimensions={0} | all-to-all | bytes 3145728 | tf_op jit(solution)/shard_map/all_to_all | solution.py:293
  654.2 2.3 copy.92
  661.2 6.5 fusion.78
  669.0 11.0 fusion.53
  680.2 42.1 %reduce-scatter.11.cloned.1.call-done = f32[328,1024]{1,0:T(8,128)} async-done(((f32[2624,1024]{1,0:T(8,128)}), f32[328,1024]{1,0:T(8,128)}) %reduce-scatter.11.cloned.1.call-update) | async-done | bytes 1343504 | tf_op jit(solution)/shard_map/reduce_scatter | solution.py:266
  722.3 129.9 %reduce-scatter.5.cloned.1.call-done = f32[128,3072]{1,0:T(8,128)} async-done(((f32[1024,3072]{1,0:T(8,128)}), f32[128,3072]{1,0:T(8,128)}) %reduce-scatter.5.cloned.1.call-update) | async-done | bytes 1572880 | tf_op jit(solution)/shard_map/reduce_scatter | solution.py:314
  852.2 213.4 %reduce-scatter.9.cloned.1.call-done = f32[128,5248]{1,0:T(8,128)} async-done(((f32[1024,5248]{1,0:T(8,128)}), f32[128,5248]{1,0:T(8,128)}) %reduce-scatter.9.cloned.1.call-update) | async-done | bytes 2686992 | tf_op jit(solution)/shard_map/reduce_scatter | solution.py:265
  1066.9 39.2 %all-reduce.8 = (f32[1]{0:T(128)}, f32[1]{0:T(128)}, f32[1]{0:T(128)}, f32[]{:T(128)}) all-reduce(f32[1]{0:T(128)} %bitcast.50, f32[1]{0:T(128)} %bitcast.49, f32[1]{0:T(128)} %bitcast.48, f32[]{:T(128)} %get-tuple-element.337), channel_id=1, replica_groups=mesh['seq'=4,'fsdp'=8] {'seq','fsdp'}, use_global_device_ids=true, to_apply=%region_34.35 | all-reduce | flops 4 | bytes 32 | tf_op jit(solution)/shard_map/psum | solution.py:221
  1106.7 2.5 fusion.82
  1109.2 5.0 fusion.62
  1115.8 16.0 %all-reduce.9 = (f32[1024]{0:T(1024)S(1)}, f32[1024]{0:T(1024)S(1)}) all-reduce(f32[1024]{0:T(1024)S(1)} %get-tuple-element.272, f32[1024]{0:T(1024)S(1)} %copy-done.36), channel_id=6, replica_groups=mesh['seq'=4,'fsdp'=8] {'fsdp'}, use_global_device_ids=true, to_apply=%region_24.25.clone | all-reduce | flops 2048 | bytes 16384
  1131.9 9.2 all-reduce.10
  1141.1 2.9 add_bitcast_fusion
  1144.0 60.8 %all-reduce.14.cloned.1.call-done = (f32[128,3072]{1,0:T(8,128)}, f32[128,1024]{1,0:T(8,128)}, f32[128,5248]{1,0:T(8,128)}, f32[328,1024]{1,0:T(8,128)}) async-done(((f32[128,3072]{1,0:T(8,128)}, f32[128,1024]{1,0:T(8,128)}, f32[128,5248]{1,0:T(8,128)}, f32[328,1024]{1,0:T(8,128)}), (f32[128,3072]{1,0:T(8,128)}, f32[128,1024]{1,0:T(8,128)}, f32[128,5248]{1,0:T(8,128)}, ...) | async-done | bytes 6127632 | tf_op jit(solution)/shard_map/psum | solution.py:318
  1204.8 2.9 copy.127
  1207.7 1.9 copy.128
  (196 shorter events, 44.1 us)
Async XLA Ops:
  7.2 17.7 %copy-start.11 = (bf16[128,5248]{1,0:T(8,128)(2,1)S(1)}, bf16[128,5248]{1,0:T(8,128)(2,1)}, u32[]{:S(2)}) copy-start(bf16[128,5248]{1,0:T(8,128)(2,1)} %param.19) | copy-start | bytes 4030468
  7.2 108.1 %all-gather.7.cloned.1.call-start = ((), (), s32[]{:S(2)}) async-start(), calls=%async_computation.8 | async-start | bytes 7077888 | tf_op jit(solution)/shard_map/all_gather | solution.py:170
  7.9 18.9 %copy-start.2 = (bf16[1,256,1024]{2,1,0:T(8,128)(2,1)S(1)}, bf16[1,256,1024]{2,1,0:T(8,128)(2,1)}, u32[]{:S(2)}) copy-start(bf16[1,256,1024]{2,1,0:T(8,128)(2,1)} %param.14) | copy-start | bytes 1572868
  7.9 296.5 %all-gather.9.cloned.1.call-start = ((), (), s32[]{:S(2)}) async-start(), calls=%async_computation.9 | async-start | bytes 2359296 | tf_op jit(solution)/shard_map/all_gather | solution.py:171
  8.7 514.9 %all-gather.11.cloned.1.call-start = ((), (), s32[]{:S(2)}) async-start(), calls=%async_computation.10 | async-start | bytes 6045696 | tf_op jit(solution)/shard_map/all_gather | solution.py:176
  9.4 523.4 %all-gather.13.cloned.1.call-start = ((), (), s32[]{:S(2)}) async-start(), calls=%async_computation.11 | async-start | bytes 12091392 | tf_op jit(solution)/shard_map/all_gather | solution.py:238
  10.0 14.9 %collective-permute-start = (bf16[128,5248]{1,0:T(8,128)(2,1)}, bf16[128,5248]{1,0:T(8,128)(2,1)S(1)}, u32[]{:S(2)}, u32[]{:S(2)}) collective-permute-start(bf16[128,5248]{1,0:T(8,128)(2,1)} %param.19), channel_id=1, source_target_pairs={{0,1},{1,0},{2,3},{3,2},{4,5},{5,4},{6,7},{7,6},{8,9},{9,8},{10,11... | collective-permute-start | bytes 4030472 | tf_op jit(solution)/shard_map/ppermute | solution.py:18
  23.7 100.3 %copy-start.26 = (f32[8,1,128]{2,1,0:T(1,128)}, f32[8,1,128]{2,1,0:T(1,128)S(1)}, u32[]{:S(2)}) copy-start(f32[8,1,128]{2,1,0:T(1,128)S(1)} %convert_element_type.149) | copy-start | bytes 12292
  26.8 109.7 %collective-permute-start.1 = (bf16[256,5248]{1,0:T(8,128)(2,1)}, bf16[256,5248]{1,0:T(8,128)(2,1)}, u32[]{:S(2)}, u32[]{:S(2)}) collective-permute-start(bf16[256,5248]{1,0:T(8,128)(2,1)} %maximum_select_fusion.3), channel_id=1, source_target_pairs={{0,2},{1,3},{2,0},{3,1},{4,6},{5,7},{6,4},{7,5},{8,10},{9,11},{10,... | collective-permute-start | bytes 8060936 | tf_op jit(solution)/shard_map/ppermute | solution.py:18
  26.9 97.1 %copy-start.28 = (f32[256]{0:T(256)}, f32[256]{0:T(256)S(1)}, u32[]{:S(2)}) copy-start(f32[256]{0:T(256)S(1)} %broadcast_multiply_fusion.1) | copy-start | bytes 3076
  27.2 96.8 %copy-start.34 = (f32[256]{0:T(256)}, f32[256]{0:T(256)S(1)}, u32[]{:S(2)}) copy-start(f32[256]{0:T(256)S(1)} %fusion.61) | copy-start | bytes 3076
  27.2 96.8 %copy-start.30 = (f32[256]{0:T(256)}, f32[256]{0:T(256)S(1)}, u32[]{:S(2)}) copy-start(f32[256]{0:T(256)S(1)} %fusion.80) | copy-start | bytes 3076
  27.4 101.7 %copy-start.22 = (f32[256,32]{0,1:T(8,128)}, f32[256,32]{0,1:T(8,128)S(1)}, u32[]{:S(2)}) copy-start(f32[256,32]{0,1:T(8,128)S(1)} %get-tuple-element.374) | copy-start | bytes 98308
  27.4 101.7 %copy-start.24 = (f32[256,32]{0,1:T(8,128)}, f32[256,32]{0,1:T(8,128)S(1)}, u32[]{:S(2)}) copy-start(f32[256,32]{0,1:T(8,128)S(1)} %get-tuple-element.375) | copy-start | bytes 98308
  129.5 6.3 copy-start.20
  130.9 23.0 %all-to-all-start = ((bf16[256,3,4,256]{0,3,1,2:T(8,128)(2,1)}), bf16[256,3,4,256]{0,3,1,2:T(8,128)(2,1)S(1)}, u32[]{:S(2)}, u32[]{:S(2)}) async-start(bf16[256,3,4,256]{0,3,1,2:T(8,128)(2,1)} %pad_maximum_fusion.3), calls=%async_computation | async-start | bytes 3145728 | tf_op jit(solution)/shard_map/all_to_all | solution.py:196
  144.3 368.4 %collective-permute-start.2 = (bf16[512,5248]{1,0:T(8,128)(2,1)}, bf16[512,5248]{1,0:T(8,128)(2,1)}, u32[]{:S(2)}, u32[]{:S(2)}) collective-permute-start(bf16[512,5248]{1,0:T(8,128)(2,1)} %maximum_select_fusion.2), channel_id=1, source_target_pairs={{0,4},{1,5},{2,6},{3,7},{4,0},{5,1},{6,2},{7,3},{8,12},{9,13},{10,... | collective-permute-start | bytes 16121864 | tf_op jit(solution)/shard_map/ppermute | solution.py:18
  156.3 6.0 copy-start.21
  178.0 16.6 %copy-start.37 = (bf16[128]{0:T(256)(128)(2,1)S(1)}, bf16[128]{0:T(256)(128)(2,1)}, u32[]{:S(2)}) copy-start(bf16[128]{0:T(256)(128)(2,1)} %param.22) | copy-start | bytes 772
  190.4 108.9 %all-to-all-start.1 = ((bf16[4,2,32768]{2,1,0:T(2,128)(2,1)}), bf16[4,2,32768]{2,1,0:T(2,128)(2,1)}, u32[]{:S(2)}, u32[]{:S(2)}) async-start(bf16[4,2,32768]{2,1,0:T(2,128)(2,1)} %reshape.507), calls=%async_computation.1 | async-start | bytes 1048576 | tf_op jit(solution)/shard_map/all_to_all | solution.py:209
  194.5 485.6 %reduce-scatter.7.cloned.1.call-start = ((), (), s32[]{:S(2)}) async-start(), calls=%async_computation.13 | async-start | bytes 4718592 | tf_op jit(solution)/shard_map/reduce_scatter | solution.py:315
  307.9 235.7 %copy-start.4 = (f32[256,1024]{1,0:T(8,128)}, f32[256,1024]{1,0:T(8,128)S(1)}, u32[]{:S(2)}) copy-start(f32[256,1024]{1,0:T(8,128)S(1)} %get-tuple-element.342) | copy-start | bytes 3145732
  512.7 10.9 copy-start.12
  532.8 6.8 copy-start.17
  532.8 6.8 copy-start.19
  532.8 7.2 copy-start.38
  540.0 5.1 copy-start.13
  543.6 1.6 copy-start.8
  544.1 1.0 copy-start.6
  544.1 4.0 copy-start.32
  548.0 1.0 copy-start.14
  548.1 174.2 %reduce-scatter.11.cloned.1.call-start = ((), (), s32[]{:S(2)}) async-start(), calls=%async_computation.15 | async-start | bytes 12091392 | tf_op jit(solution)/shard_map/reduce_scatter | solution.py:266
  559.4 12.1 all-to-all-start.2
  563.2 288.9 %reduce-scatter.5.cloned.1.call-start = ((), (), s32[]{:S(2)}) async-start(), calls=%async_computation.12 | async-start | bytes 14155776 | tf_op jit(solution)/shard_map/reduce_scatter | solution.py:314
  577.0 1.3 copy-start.9
  578.3 3.2 copy-start
  585.2 8.2 copy-start.1
  588.6 4.8 copy-start.10
  597.7 1.3 copy-start.9
  599.0 3.2 copy-start
  605.9 8.1 copy-start.1
  609.3 4.8 copy-start.10
  656.6 3.0 copy-start.23
  656.6 3.0 copy-start.25
  660.2 1.1 copy-start.3
  660.2 1.1 copy-start.27
  660.2 1.0 copy-start.29
  660.2 1.0 copy-start.31
  667.8 1.3 copy-start.5
  667.8 397.8 %reduce-scatter.9.cloned.1.call-start = ((), (), s32[]{:S(2)}) async-start(), calls=%async_computation.14 | async-start | bytes 24182784 | tf_op jit(solution)/shard_map/reduce_scatter | solution.py:265
  680.1 385.5 %copy-start.39 = (u32[32]{0:T(128)S(1)}, u32[32]{0:T(128)}, u32[]{:S(2)}) copy-start(u32[32]{0:T(128)} %constant.122) | copy-start | bytes 388
  680.1 524.7 %all-reduce.14.cloned.1.call-start = ((), (), s32[]{:S(2)}) async-start(), calls=%async_computation.16 | async-start | bytes 12255232 | tf_op jit(solution)/shard_map/psum | solution.py:318
  1109.2 5.0 copy-start.35
  1109.2 6.5 copy-start.36
  1109.2 31.9 %copy-start.7 = (f32[256,1024]{1,0:T(8,128)S(1)}, f32[256,1024]{1,0:T(8,128)}, u32[]{:S(2)}) copy-start(f32[256,1024]{1,0:T(8,128)} %copy-done.6) | copy-start | bytes 3145732
  1109.2 31.9 %copy-start.33 = (f32[256]{0:T(256)S(1)}, f32[256]{0:T(256)}, u32[]{:S(2)}) copy-start(f32[256]{0:T(256)} %copy-done.32) | copy-start | bytes 3076
  1114.2 1.0 copy-start.15
  1204.8 4.7 copy-start.16
  1204.8 6.3 copy-start.18
Sparse Core Ops, SparseCore 0:
  9.6 105.6 all-gather.6
  116.9 35.3 all-gather.8
  154.0 179.7 all-gather.10
  335.3 147.8 all-gather.12
  548.2 61.5 reduce-scatter.6
  611.9 110.2 reduce-scatter.10
  724.6 127.5 reduce-scatter.4
  854.5 210.9 reduce-scatter.8
  1069.5 135.2 all-reduce.13
